TPU v7x, 256 devices: a whole 4x4x8 slice. The times are simulated.
256 devices in a mesh: pipe: 4 (over x), seq: 16 (over z, core), chan: 4 (over y).
Axes of the slice: x: 4, y: 4, z: 8, core: 2. Of those that a mesh axis runs over, the one named last changes fastest.
Arguments:
- signal: bfloat16 [4, 4096, 2048], P('pipe', 'seq', 'chan'), may hold values from -6 to 6
- gate_value: bfloat16 [4, 4096, 2048], P('pipe', 'seq', 'chan'), may hold values from -6 to 6
- grad_out: bfloat16 [4, 4096, 2048], P('pipe', 'seq', 'chan'), may hold values from -1.5 to 1.5
- long_filter: bfloat16 [4, 4096, 2048], P('pipe', 'seq', 'chan'), may hold values from -0.09375 to 0.09375
- weight: bfloat16 [4, 4096, 2048], P('pipe', None, 'chan'), may hold values from -0.125 to 0.125
Outputs:
- gate_grad: bfloat16 [4, 4096, 2048], P('pipe', 'seq', 'chan')
- filter_grad: float32 [4, 4096, 2048], P('pipe', 'seq', 'chan')
- input_grad: bfloat16 [4, 4096, 4096], P('pipe', 'seq', 'chan')
All inputs are finite; a program needn't handle non-finite values.
Results may differ from a plain program's by a relative error of at most 0.02.
Values may be sent and summed in bfloat16 or wider, within the bound.
No kernel may reach another device: no remote copies, remote signals or barrier semaphores. Data moves between devices by JAX's collectives and lax.ppermute only.
A program may use at most 128 MiB of HBM per device.

v0:
```python
import math
import jax
import jax.numpy as jnp
from jax import lax
from jax.sharding import PartitionSpec as P

HIGHEST = lax.Precision.HIGHEST
HIGHER = lax.Precision.HIGH


def passed_along(x, axis, by):
    length = lax.axis_size(axis)
    return lax.ppermute(x, axis, [(i, (i + by) % length) for i in range(length)])


def make_tables(panel_len):
    span_len = 2 * panel_len
    row_index = lax.broadcasted_iota(jnp.int32, (span_len, panel_len), 0)
    col_index = lax.broadcasted_iota(jnp.int32, (span_len, panel_len), 1)
    frequency = jnp.where(row_index <= panel_len, row_index, row_index - panel_len)
    angles = (frequency * col_index % span_len).astype(jnp.float32) * (2.0 * math.pi / span_len)
    forward_table = jnp.where(row_index <= panel_len, jnp.cos(angles), -jnp.sin(angles))
    end_rows = jnp.logical_or(row_index == 0, row_index == panel_len)
    weights = jnp.where(end_rows, 1.0, 2.0) / span_len
    inverse_table = (forward_table * weights).T
    return (forward_table, inverse_table)


def make_parity(panel_len):
    row_index = lax.broadcasted_iota(jnp.int32, (2 * panel_len, 1), 0)
    frequency = jnp.where(row_index <= panel_len, row_index, row_index - panel_len)
    return (1 - 2 * (frequency % 2)).astype(jnp.float32)


def spec_product(left_spec, right_spec, interior, conjugate):
    panel_len = left_spec.shape[0] // 2
    left_real, left_imag = (left_spec[:panel_len], left_spec[panel_len:])
    right_real, right_imag = (right_spec[:panel_len], right_spec[panel_len:])
    if conjugate:
        right_imag = right_imag * (1.0 - 2.0 * interior)
    real_part = left_real * right_real - interior * left_imag * right_imag
    imag_part = (
        interior * (left_real * right_imag + left_imag * right_real)
        + (1.0 - interior) * left_imag * right_imag
    )
    return jnp.concatenate([real_part, imag_part], axis=0)


def on_device(signal, gate_value, grad_out, long_filter, weight):
    panel_len = signal.shape[1]
    chan_width = signal.shape[2]
    span_len = 2 * panel_len
    panel_count = lax.axis_size("seq")
    my_panel = lax.axis_index("seq")
    forward_table, inverse_table = make_tables(panel_len)
    parity = make_parity(panel_len)
    interior = (lax.broadcasted_iota(jnp.int32, (panel_len, 1), 0) != 0).astype(jnp.float32)
    gated = (gate_value[0].astype(jnp.float32) * grad_out[0].astype(jnp.float32)).astype(
        jnp.bfloat16
    )
    signals, gateds, filters = (
        lax.all_gather(signal, "seq", axis=1, tiled=True),
        lax.all_gather(gated[None], "seq", axis=1, tiled=True),
        lax.all_gather(long_filter, "seq", axis=1, tiled=True),
    )
    zero_spec = jnp.zeros((span_len, chan_width), jnp.float32)

    def spectrum(gathered, panel_at):
        panel_rows = lax.dynamic_slice_in_dim(gathered[0], panel_at * panel_len, panel_len, 0)
        return jnp.dot(forward_table, panel_rows.astype(jnp.float32), precision=HIGHER)

    def spectrum_if(use_panel, gathered, panel_at):
        return lax.cond(
            use_panel,
            lambda where_at: spectrum(gathered, where_at),
            lambda where_at: zero_spec,
            panel_at,
        )

    def invert(spectrum_in):
        return jnp.dot(inverse_table, spectrum_in, precision=HIGHEST)

    def settle(lag_parts, spectrum_in, use_panel, target):

        def add_rows(parts_now):
            row_at = jnp.maximum(target, 0)
            current = lax.dynamic_index_in_dim(parts_now, row_at, 0, keepdims=True)
            return lax.dynamic_update_index_in_dim(
                parts_now, current + invert(spectrum_in)[None], row_at, 0
            )

        return lax.cond(use_panel, add_rows, lambda parts_now: parts_now, lag_parts)

    own_gated = jnp.dot(forward_table, gated.astype(jnp.float32), precision=HIGHER)
    last_lag = jnp.maximum(my_panel, panel_count - 1 - my_panel)
    extras = (
        zero_spec,
        jnp.array(False),
        jnp.zeros((panel_count, panel_len, chan_width), jnp.float32),
    )

    def lag_step(lag_index, loop_state):
        prior_filter, forward_sum, backward_sum, extras_now = loop_state
        filter_now = spectrum(filters, lag_index)
        filter_full = filter_now + parity * prior_filter
        use_forward = lag_index <= my_panel
        use_backward = lag_index <= panel_count - 1 - my_panel
        signal_spec = spectrum_if(use_forward, signals, jnp.maximum(my_panel - lag_index, 0))
        gated_spec = spectrum_if(
            use_backward, gateds, jnp.minimum(my_panel + lag_index, panel_count - 1)
        )
        forward_sum = forward_sum + spec_product(filter_full, signal_spec, interior, False)
        backward_sum = backward_sum + spec_product(gated_spec, filter_full, interior, True)
        prior_pair, prior_flag, lag_parts = extras_now
        pair_spec = spec_product(own_gated, signal_spec, interior, True)
        ready = jnp.logical_and(lag_index >= 1, jnp.logical_or(prior_flag, use_forward))
        lag_parts = settle(lag_parts, prior_pair + parity * pair_spec, ready, lag_index - 1)
        extras_now = (pair_spec, use_forward, lag_parts)
        return (filter_now, forward_sum, backward_sum, extras_now)

    unused_filter, forward_sum, backward_sum, extras = lax.fori_loop(
        0, last_lag + 1, lag_step, (zero_spec, zero_spec, zero_spec, extras)
    )
    prior_pair, prior_flag, lag_parts = extras
    lag_parts = settle(lag_parts, prior_pair, prior_flag, last_lag)
    filter_grad = lax.psum_scatter(
        lag_parts.reshape(1, panel_count * panel_len, chan_width).astype(jnp.bfloat16),
        "seq",
        scatter_dimension=1,
        tiled=True,
    ).astype(jnp.float32)
    conv = invert(forward_sum)
    gate_grad = (grad_out[0].astype(jnp.float32) * conv).astype(jnp.bfloat16)[None]
    signal_grad = invert(backward_sum).astype(jnp.bfloat16)
    received = passed_along(signal_grad[None], "pipe", -1)
    partial_sums = lax.dot_general(
        received[0], weight[0], (((1,), (1,)), ((), ())), preferred_element_type=jnp.float32
    )
    input_grad = lax.psum_scatter(
        partial_sums[None], "chan", scatter_dimension=2, tiled=True
    ).astype(jnp.bfloat16)
    return (gate_grad, filter_grad, input_grad)


def solution(mesh):
    return jax.shard_map(
        on_device,
        mesh=mesh,
        in_specs=(
            P("pipe", "seq", "chan"),
            P("pipe", "seq", "chan"),
            P("pipe", "seq", "chan"),
            P("pipe", "seq", "chan"),
            P("pipe", None, "chan"),
        ),
        out_specs=(P("pipe", "seq", "chan"), P("pipe", "seq", "chan"), P("pipe", "seq", "chan")),
        check_vma=False,
    )
```

profile of v0, /device:TPU:1, one launch (start us, length us, event | category | flops | bytes accessed | tf_op | source)
XLA Modules:
  0.0 692.9 jit_solution(5440354241216987989)
XLA Ops:
  11.7 4.8 fusion.62
  16.4 40.3 %all-gather.8.cloned.1.call-done = bf16[1,4096,512]{2,1,0:T(8,128)(2,1)} async-done(((bf16[1,256,512]{2,1,0:T(8,128)(2,1)}), bf16[1,4096,512]{2,1,0:T(8,128)(2,1)}) %all-gather.8.cloned.1.call-update) | async-done | bytes 4194320 | tf_op jit(solution)/shard_map/all_gather | solution.py:63
  56.8 42.5 %all-gather.4.cloned.1.call-done = bf16[1,4096,512]{2,1,0:T(8,128)(2,1)} async-done(((bf16[1,256,512]{2,1,0:T(8,128)(2,1)}), bf16[1,4096,512]{2,1,0:T(8,128)(2,1)}) %all-gather.4.cloned.1.call-update) | async-done | bytes 4194320 | tf_op jit(solution)/shard_map/all_gather | solution.py:64
  99.3 42.5 %all-gather.6.cloned.1.call-done = bf16[1,4096,512]{2,1,0:T(8,128)(2,1)} async-done(((bf16[1,256,512]{2,1,0:T(8,128)(2,1)}), bf16[1,4096,512]{2,1,0:T(8,128)(2,1)}) %all-gather.6.cloned.1.call-update) | async-done | bytes 4194320 | tf_op jit(solution)/shard_map/all_gather | solution.py:62
  141.8 4.1 broadcast_in_dim.38
  149.6 290.2 %while.31 = (s32[]{:T(128)}, f32[512,512]{1,0:T(8,128)S(1)}, f32[512,512]{1,0:T(8,128)}, f32[512,512]{1,0:T(8,128)}, f32[512,512]{1,0:T(8,128)}, /*index=5*/pred...) while((s32[]{:T(128)}, f32[512,512]{1,0:T(8,128)S(1)}, ...), condition=%wide.region_7.8_spmd.clone.clone.clone, body=%wide.region_0.7_spmd.clone.clone.clone.sunk | while | flops 2027169536 | bytes 49307344 | solution.py:121
  149.6 4.7 multiply_add_fusion.5
  165.9 3.6 maximum_add_fusion.3
  169.6 4.7 multiply_add_fusion.5
  184.9 7.4 %conditional.19 = (f32[16,256,512]{1,2,0:T(8,128)}) conditional(s32[]{:T(128)} %convert_element_type.270, f32[16,256,512]{1,2,0:T(8,128)} %get-tuple-element.824, (s32[]{:T(128)}, f32[16,256,512]{1,2,0:T(8,128)}, f32[512,1]{0,1:T(1,128)S(1)}, f32[512,512]{1,0:T(8,128)S(1)}, f32[512,512]{1,0:T(8,128)}, /*index=5*/pred[256,512]{1,0:T(32,128)(4,1)S(1)}, ...), branch_computations={%region_5.5_spmd, %region_6.6_spmd} | conditional | flops 806354944 | bytes 4329508 | solution.py:92
  184.9 7.4 %fusion.15 = f32[16,256,512]{1,2,0:T(8,128)} fusion(f32[16,256,512]{1,2,0:T(8,128)} %get-tuple-element.344, s32[]{:T(128)S(6)} %max.13, f32[512,512]{1,0:T(8,128)} %get-tuple-element.346, f32[512,512]{1,0:T(8,128)S(1)} %get-tuple-element.348, pred[256,512]{1,0:T(32,128)(4,1)S(1)} %get-tuple-element.581, f32[256,512]{1,0:T(8,128)S(1)} %get-tuple-element.587, ...), kind=kOutput, calls=%fused_computation.14 | convolution fusion | flops 806354944 | bytes 4329476 | tf_op jit(solution)/shard_map/while/body/cond/branch_1_fun/dot_general | solution.py:81
  193.3 3.6 maximum_add_fusion.3
  196.9 4.7 multiply_add_fusion.5
  210.3 7.4 %conditional.19 = (f32[16,256,512]{1,2,0:T(8,128)}) conditional(s32[]{:T(128)} %convert_element_type.270, f32[16,256,512]{1,2,0:T(8,128)} %get-tuple-element.824, (s32[]{:T(128)}, f32[16,256,512]{1,2,0:T(8,128)}, f32[512,1]{0,1:T(1,128)S(1)}, f32[512,512]{1,0:T(8,128)S(1)}, f32[512,512]{1,0:T(8,128)}, /*index=5*/pred[256,512]{1,0:T(32,128)(4,1)S(1)}, ...), branch_computations={%region_5.5_spmd, %region_6.6_spmd} | conditional | flops 806354944 | bytes 4329508 | solution.py:92
  210.4 7.4 %fusion.15 = f32[16,256,512]{1,2,0:T(8,128)} fusion(f32[16,256,512]{1,2,0:T(8,128)} %get-tuple-element.344, s32[]{:T(128)S(6)} %max.13, f32[512,512]{1,0:T(8,128)} %get-tuple-element.346, f32[512,512]{1,0:T(8,128)S(1)} %get-tuple-element.348, pred[256,512]{1,0:T(32,128)(4,1)S(1)} %get-tuple-element.581, f32[256,512]{1,0:T(8,128)S(1)} %get-tuple-element.587, ...), kind=kOutput, calls=%fused_computation.14 | convolution fusion | flops 806354944 | bytes 4329476 | tf_op jit(solution)/shard_map/while/body/cond/branch_1_fun/dot_general | solution.py:81
  218.8 3.6 maximum_add_fusion.3
  222.4 4.7 multiply_add_fusion.5
  236.9 3.6 maximum_add_fusion.3
  240.6 4.7 multiply_add_fusion.5
  255.0 3.6 maximum_add_fusion.3
  258.7 4.7 multiply_add_fusion.5
  273.1 3.6 maximum_add_fusion.3
  276.8 4.7 multiply_add_fusion.5
  291.2 3.6 maximum_add_fusion.3
  294.9 4.7 multiply_add_fusion.5
  309.3 3.6 maximum_add_fusion.3
  313.0 4.7 multiply_add_fusion.5
  327.4 3.6 maximum_add_fusion.3
  331.1 4.7 multiply_add_fusion.5
  345.6 3.6 maximum_add_fusion.3
  349.2 4.7 multiply_add_fusion.5
  363.7 3.6 maximum_add_fusion.3
  367.3 4.7 multiply_add_fusion.5
  381.8 3.6 maximum_add_fusion.3
  385.4 4.7 multiply_add_fusion.5
  399.9 3.6 maximum_add_fusion.3
  403.5 4.7 multiply_add_fusion.5
  418.0 3.6 maximum_add_fusion.3
  421.6 4.7 multiply_add_fusion.5
  436.1 3.6 maximum_add_fusion.3
  439.8 9.3 %conditional.4 = (f32[16,256,512]{2,1,0:T(8,128)}) conditional(s32[]{:T(128)} %convert_element_type.151, (f32[16,256,512]{1,2,0:T(8,128)}) %tuple.109, (s32[]{:T(128)}, f32[16,256,512]{1,2,0:T(8,128)}, pred[256,512]{1,0:T(32,128)(4,1)S(1)}, f32[512,512]{1,0:T(8,128)}, f32[512]{0:T(512)S(1)}, /*index=5*/f32[256,512]{1,0:T(8,128)}, ...), branch_computations={%region_8.9_spmd, %region_9.10_spmd} | conditional | flops 805830656 | bytes 26347600 | solution.py:92
  439.8 9.2 %copy.46 = f32[16,256,512]{2,1,0:T(8,128)} copy(f32[16,256,512]{1,2,0:T(8,128)} %get-tuple-element.589) | data formatting | bytes 16777216 | tf_op jit(solution)/shard_map/while | solution.py:121
  449.0 5.9 convert_element_type.152
  462.2 3.3 collective-permute-done
  465.5 5.5 convolution_bitcast_fusion.5
  472.3 4.0 fusion.50
  476.2 154.6 %reduce-scatter.3.cloned.1.call-done = bf16[1,256,512]{2,1,0:T(8,128)(2,1)} async-done(((bf16[1,4096,512]{2,1,0:T(8,128)(2,1)}), bf16[1,256,512]{2,1,0:T(8,128)(2,1)}) %reduce-scatter.3.cloned.1.call-update) | async-done | bytes 262160 | tf_op jit(solution)/shard_map/reduce_scatter | solution.py:126
  632.7 51.6 %reduce-scatter.5.cloned.1.call-done = f32[1,256,1024]{2,1,0:T(8,128)} async-done(((f32[1,256,4096]{2,1,0:T(8,128)}), f32[1,256,1024]{2,1,0:T(8,128)}) %reduce-scatter.5.cloned.1.call-update) | async-done | bytes 1048592 | tf_op jit(solution)/shard_map/reduce_scatter | solution.py:139
  (392 shorter events, 204.1 us)
Async XLA Ops:
  7.2 49.6 %all-gather.8.cloned.1.call-start = ((), (), s32[]{:S(2)}) async-start(), calls=%async_computation.4 | async-start | bytes 4456448 | tf_op jit(solution)/shard_map/all_gather | solution.py:63
  9.0 90.3 %all-gather.4.cloned.1.call-start = ((), (), s32[]{:S(2)}) async-start(), calls=%async_computation.2 | async-start | bytes 4456448 | tf_op jit(solution)/shard_map/all_gather | solution.py:64
  9.8 132.1 %all-gather.6.cloned.1.call-start = ((), (), s32[]{:S(2)}) async-start(), calls=%async_computation.3 | async-start | bytes 4456448 | tf_op jit(solution)/shard_map/all_gather | solution.py:62
  10.5 620.3 %reduce-scatter.3.cloned.1.call-start = ((), (), s32[]{:S(2)}) async-start(), calls=%async_computation.5 | async-start | bytes 4456448 | tf_op jit(solution)/shard_map/reduce_scatter | solution.py:126
  154.3 2.2 copy-start.5
  160.5 0.8 copy-start
  165.9 3.6 copy-start.6
  174.2 2.2 copy-start.5
  180.5 0.8 copy-start
  193.3 3.6 copy-start.6
  201.6 2.2 copy-start.5
  206.0 0.8 copy-start
  218.8 3.6 copy-start.6
  227.1 2.2 copy-start.5
  231.5 0.8 copy-start
  236.9 3.6 copy-start.6
  245.2 2.2 copy-start.5
  255.0 3.6 copy-start.6
  263.3 2.2 copy-start.5
  267.7 0.8 copy-start
  273.1 3.6 copy-start.6
  281.4 2.2 copy-start.5
  291.2 3.6 copy-start.6
  299.5 2.2 copy-start.5
  309.3 3.6 copy-start.6
  317.6 2.2 copy-start.5
  327.4 3.6 copy-start.6
  335.8 2.2 copy-start.5
  340.1 0.8 copy-start
  345.6 3.6 copy-start.6
  353.9 2.2 copy-start.5
  358.2 0.8 copy-start
  363.7 3.6 copy-start.6
  372.0 2.2 copy-start.5
  381.8 3.6 copy-start.6
  390.1 2.2 copy-start.5
  394.5 0.8 copy-start
  399.9 3.6 copy-start.6
  408.2 2.2 copy-start.5
  418.0 3.6 copy-start.6
  426.3 2.2 copy-start.5
  430.7 0.8 copy-start
  436.1 3.6 copy-start.6
  455.0 1.2 copy-start.3
  455.0 229.3 %reduce-scatter.5.cloned.1.call-start = ((), (), s32[]{:S(2)}) async-start(), calls=%async_computation.6 | async-start | bytes 5242880 | tf_op jit(solution)/shard_map/reduce_scatter | solution.py:139
  459.5 6.0 collective-permute-start
  471.0 1.2 copy-start.2
  471.0 1.3 copy-start.7
  (6 other events, 4.8 us)
Sparse Core Ops, SparseCore 0:
  10.4 46.3 all-gather.7
  58.6 40.6 all-gather.3
  101.1 40.6 all-gather.5
  455.1 175.7 reduce-scatter.2
  633.3 50.9 reduce-scatter.4
where the time goes:
time: 695 us; the launch traced here: 693 us
  waiting for transfers between devices  336 us (48%)
  other arithmetic  153 us (22%)
  matrix products  127 us (18%)
  local copies, waits for them, and re-layouts  56.4 us (8%)
  between operations  13.8 us (2%)
    reduce_scatter x1, waiting for transfers between devices, on_device(): lax.psum_scatter(lag_parts.reshape(1, panel_count * panel_len, chan_width...  155 us
    dot_general x32, matrix products, spectrum(): jnp.dot(forward_table, panel_rows.astype(jnp.float32), precision=HIGHER)  95.2 us
    add x15, other arithmetic, lag_step(): forward_sum + spec_product(filter_full, signal_spec, interior, False)  54.5 us
    reduce_scatter x1, waiting for transfers between devices, on_device(): lax.psum_scatter(partial_sums[None], 'chan', scatter_dimension=2, tiled=T...  51.6 us
    sub x15, other arithmetic, spec_product(): real_part = left_real * right_real - interior * left_imag * right_imag  47.5 us
    all_gather x1, waiting for transfers between devices, on_device(): lax.all_gather(signal, 'seq', axis=1, tiled=True)  42.5 us
    all_gather x1, waiting for transfers between devices, on_device(): lax.all_gather(long_filter, 'seq', axis=1, tiled=True)  42.5 us
    all_gather x1, waiting for transfers between devices, on_device(): lax.all_gather(gated[None], 'seq', axis=1, tiled=True)  40.3 us
  transfers between devices with their start and end apart: 6, of which 6 were waited for; matrix products, arithmetic and copies ran while one was open for 3% of the time, Pallas kernels for 0%

commit v1 on v0

--- a/solution.py
+++ b/solution.py
@@ -6,6 +6,27 @@
 
 HIGHEST = lax.Precision.HIGHEST
 HIGHER = lax.Precision.HIGH
+
+
+def collect(shard, axis, dim):
+    count, position, span = (lax.axis_size(axis), lax.axis_index(axis), shard.shape[dim])
+    right = [(i, (i + 1) % count) for i in range(count)]
+    downward = [(i, (i - 1) % count) for i in range(count)]
+    result = jnp.zeros((*shard.shape[:dim], count * span, *shard.shape[dim + 1 :]), shard.dtype)
+    result = lax.dynamic_update_slice_in_dim(result, shard, position * span, axis=dim)
+    from_left = from_right = shard
+    halfway = count // 2
+    for step in range(1, halfway + 1):
+        from_left = lax.ppermute(from_left, axis, right)
+        result = lax.dynamic_update_slice_in_dim(
+            result, from_left, (position - step) % count * span, axis=dim
+        )
+        if step < count - halfway:
+            from_right = lax.ppermute(from_right, axis, downward)
+            result = lax.dynamic_update_slice_in_dim(
+                result, from_right, (position + step) % count * span, axis=dim
+            )
+    return result
 
 
 def passed_along(x, axis, by):
@@ -61,7 +82,7 @@
     signals, gateds, filters = (
         lax.all_gather(signal, "seq", axis=1, tiled=True),
         lax.all_gather(gated[None], "seq", axis=1, tiled=True),
-        lax.all_gather(long_filter, "seq", axis=1, tiled=True),
+        collect(long_filter, "seq", 1),
     )
     zero_spec = jnp.zeros((span_len, chan_width), jnp.float32)
 

time: 695 us -> 655 us (0.942)
  waiting for transfers between devices: 336 us -> 252 us
  starting transfers between devices: 2.92 us -> 34 us
  local copies, waits for them, and re-layouts: 56.4 us -> 69.1 us
    all_gather x1 -> x0, waiting for transfers between devices: 42.5 us -> none  [on_device(): lax.all_gather(long_filter, 'seq', axis=1, tiled=True)]
    all_gather x1, waiting for transfers between devices: 40.3 us -> 0.01 us  [on_device(): lax.all_gather(gated[None], 'seq', axis=1, tiled=True)]
    ppermute x0 -> x15, starting transfers between devices: none -> 31.4 us  [the longest x7 25.1 us: collect(): from_right = lax.ppermute(from_right, axis, downward)]
    ppermute x0 -> x15, waiting for transfers between devices: none -> 14.9 us  [the longest x7 7.61 us: collect(): from_right = lax.ppermute(from_right, axis, downward)]
    all_gather x1, waiting for transfers between devices: 42.5 us -> 27.7 us  [on_device(): lax.all_gather(signal, 'seq', axis=1, tiled=True)]
    dynamic_update_slice x0 -> x16, local copies, waits for them, and re-layouts: none -> 11.6 us  [the longest x8 5.76 us: collect(): lax.dynamic_update_slice_in_dim(result, from_left, (position - step) % co...]
  transfers between devices with their start and end apart: 6 -> 20, of which waited for: 6 -> 10; matrix products, arithmetic and copies ran while one was open for 3% -> 5% of each run, Pallas kernels for 0% -> 0%
where the time goes in v1:
time: 655 us; the launch traced here: 652 us
  waiting for transfers between devices  252 us (38%)
  other arithmetic  153 us (23%)
  matrix products  127 us (19%)
  local copies, waits for them, and re-layouts  69.1 us (11%)
  starting transfers between devices  34 us (5%)
  between operations  13.9 us (2%)
    reduce_scatter x1, waiting for transfers between devices, on_device(): lax.psum_scatter(lag_parts.reshape(1, panel_count * panel_len, chan_width...  154 us
    dot_general x32, matrix products, spectrum(): jnp.dot(forward_table, panel_rows.astype(jnp.float32), precision=HIGHER)  94.8 us
    add x15, other arithmetic, lag_step(): forward_sum + spec_product(filter_full, signal_spec, interior, False)  54.6 us
    reduce_scatter x1, waiting for transfers between devices, on_device(): lax.psum_scatter(partial_sums[None], 'chan', scatter_dimension=2, tiled=T...  51.7 us
    sub x15, other arithmetic, spec_product(): real_part = left_real * right_real - interior * left_imag * right_imag  47.5 us
    select_n x15, other arithmetic, make_tables(): jnp.where(row_index <= panel_len, jnp.cos(angles), -jnp.sin(angles))  33 us
    all_gather x1, waiting for transfers between devices, on_device(): lax.all_gather(signal, 'seq', axis=1, tiled=True)  27.7 us
    while x105, local copies, waits for them, and re-layouts  26 us
  transfers between devices with their start and end apart: 20, of which 10 were waited for; matrix products, arithmetic and copies ran while one was open for 5% of the time, Pallas kernels for 0%

profile of v1, /device:TPU:1, one launch (start us, length us, event | category | flops | bytes accessed | tf_op | source)
XLA Modules:
  0.0 652.5 jit_solution(1543392495552423793)
XLA Ops:
  20.9 4.8 fusion.62
  26.8 3.8 collective-permute-start.5
  37.1 4.4 collective-permute-start.7
  47.0 6.4 collective-permute-start.9
  57.6 3.8 collective-permute-start.11
  63.5 4.8 collective-permute-start.13
  71.2 3.9 collective-permute-done.14
  75.9 27.7 %all-gather.3.cloned.1.call-done = bf16[1,4096,512]{2,1,0:T(8,128)(2,1)} async-done(((bf16[1,256,512]{2,1,0:T(8,128)(2,1)}), bf16[1,4096,512]{2,1,0:T(8,128)(2,1)}) %all-gather.3.cloned.1.call-update) | async-done | bytes 4194320 | tf_op jit(solution)/shard_map/all_gather | solution.py:83
  103.6 4.2 broadcast_in_dim.41
  111.2 289.0 %while.31 = (s32[]{:T(128)}, f32[512,512]{1,0:T(8,128)S(1)}, f32[512,512]{1,0:T(8,128)}, f32[512,512]{1,0:T(8,128)}, f32[512,512]{1,0:T(8,128)}, /*index=5*/pred...) while((s32[]{:T(128)}, f32[512,512]{1,0:T(8,128)S(1)}, ...), condition=%wide.region_7.8_spmd.clone.clone.clone, body=%wide.region_0.7_spmd.clone.clone.clone.sunk | while | flops 2027169536 | bytes 49307344 | solution.py:142
  111.2 4.6 multiply_add_fusion.5
  127.5 3.6 maximum_add_fusion.3
  131.1 4.6 multiply_add_fusion.5
  146.4 7.4 %conditional.19 = (f32[16,256,512]{1,2,0:T(8,128)}) conditional(s32[]{:T(128)} %convert_element_type.270, f32[16,256,512]{1,2,0:T(8,128)} %get-tuple-element.824, (s32[]{:T(128)}, f32[16,256,512]{1,2,0:T(8,128)}, f32[512,1]{0,1:T(1,128)S(1)}, f32[512,512]{1,0:T(8,128)S(1)}, f32[512,512]{1,0:T(8,128)}, /*index=5*/pred[256,512]{1,0:T(32,128)(4,1)S(1)}, ...), branch_computations={%region_5.5_spmd, %region_6.6_spmd} | conditional | flops 806354944 | bytes 4329508 | solution.py:113
  146.4 7.4 %fusion.15 = f32[16,256,512]{1,2,0:T(8,128)} fusion(f32[16,256,512]{1,2,0:T(8,128)} %get-tuple-element.344, s32[]{:T(128)S(6)} %max.13, f32[512,512]{1,0:T(8,128)} %get-tuple-element.346, f32[512,512]{1,0:T(8,128)S(1)} %get-tuple-element.348, pred[256,512]{1,0:T(32,128)(4,1)S(1)} %get-tuple-element.581, f32[256,512]{1,0:T(8,128)S(1)} %get-tuple-element.587, ...), kind=kOutput, calls=%fused_computation.14 | convolution fusion | flops 806354944 | bytes 4329476 | tf_op jit(solution)/shard_map/while/body/cond/branch_1_fun/dot_general | solution.py:102
  154.8 3.6 maximum_add_fusion.3
  158.4 4.6 multiply_add_fusion.5
  171.8 7.4 %conditional.19 = (f32[16,256,512]{1,2,0:T(8,128)}) conditional(s32[]{:T(128)} %convert_element_type.270, f32[16,256,512]{1,2,0:T(8,128)} %get-tuple-element.824, (s32[]{:T(128)}, f32[16,256,512]{1,2,0:T(8,128)}, f32[512,1]{0,1:T(1,128)S(1)}, f32[512,512]{1,0:T(8,128)S(1)}, f32[512,512]{1,0:T(8,128)}, /*index=5*/pred[256,512]{1,0:T(32,128)(4,1)S(1)}, ...), branch_computations={%region_5.5_spmd, %region_6.6_spmd} | conditional | flops 806354944 | bytes 4329508 | solution.py:113
  171.8 7.4 %fusion.15 = f32[16,256,512]{1,2,0:T(8,128)} fusion(f32[16,256,512]{1,2,0:T(8,128)} %get-tuple-element.344, s32[]{:T(128)S(6)} %max.13, f32[512,512]{1,0:T(8,128)} %get-tuple-element.346, f32[512,512]{1,0:T(8,128)S(1)} %get-tuple-element.348, pred[256,512]{1,0:T(32,128)(4,1)S(1)} %get-tuple-element.581, f32[256,512]{1,0:T(8,128)S(1)} %get-tuple-element.587, ...), kind=kOutput, calls=%fused_computation.14 | convolution fusion | flops 806354944 | bytes 4329476 | tf_op jit(solution)/shard_map/while/body/cond/branch_1_fun/dot_general | solution.py:102
  180.2 3.6 maximum_add_fusion.3
  183.9 4.6 multiply_add_fusion.5
  198.2 3.6 maximum_add_fusion.3
  201.9 4.6 multiply_add_fusion.5
  216.2 3.6 maximum_add_fusion.3
  219.9 4.6 multiply_add_fusion.5
  234.3 3.6 maximum_add_fusion.3
  237.9 4.6 multiply_add_fusion.5
  252.3 3.6 maximum_add_fusion.3
  256.0 4.6 multiply_add_fusion.5
  270.3 3.6 maximum_add_fusion.3
  274.0 4.6 multiply_add_fusion.5
  288.4 3.6 maximum_add_fusion.3
  292.0 4.6 multiply_add_fusion.5
  306.4 3.6 maximum_add_fusion.3
  310.0 4.6 multiply_add_fusion.5
  324.4 3.6 maximum_add_fusion.3
  328.1 4.6 multiply_add_fusion.5
  346.1 4.6 multiply_add_fusion.5
  364.1 4.6 multiply_add_fusion.5
  382.2 4.6 multiply_add_fusion.5
  396.5 3.6 maximum_add_fusion.3
  400.2 9.3 %conditional.4 = (f32[16,256,512]{2,1,0:T(8,128)}) conditional(s32[]{:T(128)} %convert_element_type.151, (f32[16,256,512]{1,2,0:T(8,128)}) %tuple.109, (s32[]{:T(128)}, f32[16,256,512]{1,2,0:T(8,128)}, pred[256,512]{1,0:T(32,128)(4,1)S(1)}, f32[512,512]{1,0:T(8,128)}, f32[512]{0:T(512)S(1)}, /*index=5*/f32[256,512]{1,0:T(8,128)}, ...), branch_computations={%region_8.9_spmd, %region_9.10_spmd} | conditional | flops 805830656 | bytes 26347600 | solution.py:113
  400.2 9.2 %copy.46 = f32[16,256,512]{2,1,0:T(8,128)} copy(f32[16,256,512]{1,2,0:T(8,128)} %get-tuple-element.589) | data formatting | bytes 16777216 | tf_op jit(solution)/shard_map/while | solution.py:142
  409.5 5.9 convert_element_type.152
  425.6 5.5 convolution_bitcast_fusion.5
  432.4 4.0 fusion.50
  436.4 154.0 %reduce-scatter.3.cloned.1.call-done = bf16[1,256,512]{2,1,0:T(8,128)(2,1)} async-done(((bf16[1,4096,512]{2,1,0:T(8,128)(2,1)}), bf16[1,256,512]{2,1,0:T(8,128)(2,1)}) %reduce-scatter.3.cloned.1.call-update) | async-done | bytes 262160 | tf_op jit(solution)/shard_map/reduce_scatter | solution.py:147
  592.2 51.7 %reduce-scatter.5.cloned.1.call-done = f32[1,256,1024]{2,1,0:T(8,128)} async-done(((f32[1,256,4096]{2,1,0:T(8,128)}), f32[1,256,1024]{2,1,0:T(8,128)}) %reduce-scatter.5.cloned.1.call-update) | async-done | bytes 1048592 | tf_op jit(solution)/shard_map/reduce_scatter | solution.py:160
  (438 shorter events, 249.3 us)
Async XLA Ops:
  7.2 68.7 %all-gather.5.cloned.1.call-start = ((), (), s32[]{:S(2)}) async-start(), calls=%async_computation.3 | async-start | bytes 4456448 | tf_op jit(solution)/shard_map/all_gather | solution.py:84
  9.0 23.8 %copy-start.8 = (bf16[1,256,512]{2,1,0:T(8,128)(2,1)S(1)}, bf16[1,256,512]{2,1,0:T(8,128)(2,1)}, u32[]{:S(2)}) copy-start(bf16[1,256,512]{2,1,0:T(8,128)(2,1)} %param.18) | copy-start | bytes 786436
  9.0 94.5 %all-gather.3.cloned.1.call-start = ((), (), s32[]{:S(2)}) async-start(), calls=%async_computation.2 | async-start | bytes 4456448 | tf_op jit(solution)/shard_map/all_gather | solution.py:83
  9.8 580.6 %reduce-scatter.3.cloned.1.call-start = ((), (), s32[]{:S(2)}) async-start(), calls=%async_computation.4 | async-start | bytes 4456448 | tf_op jit(solution)/shard_map/reduce_scatter | solution.py:147
  9.8 6.7 %collective-permute-start = (bf16[1,256,512]{2,1,0:T(8,128)(2,1)}, bf16[1,256,512]{2,1,0:T(8,128)(2,1)S(1)}, u32[]{:S(2)}, u32[]{:S(2)}) collective-permute-start(bf16[1,256,512]{2,1,0:T(8,128)(2,1)} %param.18), channel_id=1, source_target_pairs={{0,4},{4,8},{8,12},{12,16},{16,20},{20,24},{24,28},{28,32},{32,36}... | collective-permute-start | bytes 786440 | tf_op jit(solution)/shard_map/ppermute | solution.py:20
  12.9 6.3 collective-permute-start.1
  16.5 9.2 %collective-permute-start.2 = (bf16[1,256,512]{2,1,0:T(8,128)(2,1)S(1)}, bf16[1,256,512]{2,1,0:T(8,128)(2,1)S(1)}, u32[]{:S(2)}, u32[]{:S(2)}) collective-permute-start(bf16[1,256,512]{2,1,0:T(8,128)(2,1)S(1)} %collective-permute-done), channel_id=1, source_target_pairs={{0,4},{4,8},{8,12},{12,16},{16,20},{20,24},{24,28},{28,32},{32,36}... | collective-permute-start | bytes 786440 | tf_op jit(solution)/shard_map/ppermute | solution.py:20
  19.2 7.6 %collective-permute-start.3 = (bf16[1,256,512]{2,1,0:T(8,128)(2,1)S(1)}, bf16[1,256,512]{2,1,0:T(8,128)(2,1)S(1)}, u32[]{:S(2)}, u32[]{:S(2)}) collective-permute-start(bf16[1,256,512]{2,1,0:T(8,128)(2,1)S(1)} %collective-permute-done.1), channel_id=1, source_target_pairs={{0,60},{4,0},{8,4},{12,8},{16,12},{20,16},{24,20},{28,24},{32,28},... | collective-permute-start | bytes 786440 | tf_op jit(solution)/shard_map/ppermute | solution.py:25
  25.7 7.9 %collective-permute-start.4 = (bf16[1,256,512]{2,1,0:T(8,128)(2,1)S(1)}, bf16[1,256,512]{2,1,0:T(8,128)(2,1)S(1)}, u32[]{:S(2)}, u32[]{:S(2)}) collective-permute-start(bf16[1,256,512]{2,1,0:T(8,128)(2,1)S(1)} %collective-permute-done.2), channel_id=1, source_target_pairs={{0,4},{4,8},{8,12},{12,16},{16,20},{20,24},{24,28},{28,32},{32,36}... | collective-permute-start | bytes 786440 | tf_op jit(solution)/shard_map/ppermute | solution.py:20
  26.8 10.4 %collective-permute-start.5 = (bf16[1,256,512]{2,1,0:T(8,128)(2,1)S(1)}, bf16[1,256,512]{2,1,0:T(8,128)(2,1)S(1)}, u32[]{:S(2)}, u32[]{:S(2)}) collective-permute-start(bf16[1,256,512]{2,1,0:T(8,128)(2,1)S(1)} %collective-permute-done.3), channel_id=1, source_target_pairs={{0,60},{4,0},{8,4},{12,8},{16,12},{20,16},{24,20},{28,24},{32,28},... | collective-permute-start | bytes 786440 | tf_op jit(solution)/shard_map/ppermute | solution.py:25
  33.6 8.7 %collective-permute-start.6 = (bf16[1,256,512]{2,1,0:T(8,128)(2,1)S(1)}, bf16[1,256,512]{2,1,0:T(8,128)(2,1)S(1)}, u32[]{:S(2)}, u32[]{:S(2)}) collective-permute-start(bf16[1,256,512]{2,1,0:T(8,128)(2,1)S(1)} %collective-permute-done.4), channel_id=1, source_target_pairs={{0,4},{4,8},{8,12},{12,16},{16,20},{20,24},{24,28},{28,32},{32,36}... | collective-permute-start | bytes 786440 | tf_op jit(solution)/shard_map/ppermute | solution.py:20
  37.1 9.8 %collective-permute-start.7 = (bf16[1,256,512]{2,1,0:T(8,128)(2,1)S(1)}, bf16[1,256,512]{2,1,0:T(8,128)(2,1)S(1)}, u32[]{:S(2)}, u32[]{:S(2)}) collective-permute-start(bf16[1,256,512]{2,1,0:T(8,128)(2,1)S(1)} %collective-permute-done.5), channel_id=1, source_target_pairs={{0,60},{4,0},{8,4},{12,8},{16,12},{20,16},{24,20},{28,24},{32,28},... | collective-permute-start | bytes 786440 | tf_op jit(solution)/shard_map/ppermute | solution.py:25
  42.2 11.8 %collective-permute-start.8 = (bf16[1,256,512]{2,1,0:T(8,128)(2,1)S(1)}, bf16[1,256,512]{2,1,0:T(8,128)(2,1)S(1)}, u32[]{:S(2)}, u32[]{:S(2)}) collective-permute-start(bf16[1,256,512]{2,1,0:T(8,128)(2,1)S(1)} %collective-permute-done.6), channel_id=1, source_target_pairs={{0,4},{4,8},{8,12},{12,16},{16,20},{20,24},{24,28},{28,32},{32,36}... | collective-permute-start | bytes 786440 | tf_op jit(solution)/shard_map/ppermute | solution.py:20
  47.0 10.6 %collective-permute-start.9 = (bf16[1,256,512]{2,1,0:T(8,128)(2,1)S(1)}, bf16[1,256,512]{2,1,0:T(8,128)(2,1)S(1)}, u32[]{:S(2)}, u32[]{:S(2)}) collective-permute-start(bf16[1,256,512]{2,1,0:T(8,128)(2,1)S(1)} %collective-permute-done.7), channel_id=1, source_target_pairs={{0,60},{4,0},{8,4},{12,8},{16,12},{20,16},{24,20},{28,24},{32,28},... | collective-permute-start | bytes 786440 | tf_op jit(solution)/shard_map/ppermute | solution.py:25
  54.1 8.0 %collective-permute-start.10 = (bf16[1,256,512]{2,1,0:T(8,128)(2,1)S(1)}, bf16[1,256,512]{2,1,0:T(8,128)(2,1)S(1)}, u32[]{:S(2)}, u32[]{:S(2)}) collective-permute-start(bf16[1,256,512]{2,1,0:T(8,128)(2,1)S(1)} %collective-permute-done.8), channel_id=1, source_target_pairs={{0,4},{4,8},{8,12},{12,16},{16,20},{20,24},{24,28},{28,32},{32,36}... | collective-permute-start | bytes 786440 | tf_op jit(solution)/shard_map/ppermute | solution.py:20
  57.6 6.0 collective-permute-start.11
  62.1 7.0 %collective-permute-start.12 = (bf16[1,256,512]{2,1,0:T(8,128)(2,1)S(1)}, bf16[1,256,512]{2,1,0:T(8,128)(2,1)S(1)}, u32[]{:S(2)}, u32[]{:S(2)}) collective-permute-start(bf16[1,256,512]{2,1,0:T(8,128)(2,1)S(1)} %collective-permute-done.10), channel_id=1, source_target_pairs={{0,4},{4,8},{8,12},{12,16},{16,20},{20,24},{24,28},{28,32},{32,36}... | collective-permute-start | bytes 786440 | tf_op jit(solution)/shard_map/ppermute | solution.py:20
  63.5 7.0 %collective-permute-start.13 = (bf16[1,256,512]{2,1,0:T(8,128)(2,1)S(1)}, bf16[1,256,512]{2,1,0:T(8,128)(2,1)S(1)}, u32[]{:S(2)}, u32[]{:S(2)}) collective-permute-start(bf16[1,256,512]{2,1,0:T(8,128)(2,1)S(1)} %collective-permute-done.11), channel_id=1, source_target_pairs={{0,60},{4,0},{8,4},{12,8},{16,12},{20,16},{24,20},{28,24},{32,28},... | collective-permute-start | bytes 786440 | tf_op jit(solution)/shard_map/ppermute | solution.py:25
  69.1 6.1 collective-permute-start.14
  115.9 2.2 copy-start.5
  127.5 3.6 copy-start.6
  154.8 3.6 copy-start.6
  163.1 2.2 copy-start.5
  180.2 3.6 copy-start.6
  188.5 2.2 copy-start.5
  198.2 3.6 copy-start.6
  206.5 2.2 copy-start.5
  216.2 3.6 copy-start.6
  224.5 2.2 copy-start.5
  234.3 3.6 copy-start.6
  242.6 2.2 copy-start.5
  252.3 3.6 copy-start.6
  260.6 2.2 copy-start.5
  270.3 3.6 copy-start.6
  278.6 2.2 copy-start.5
  288.4 3.6 copy-start.6
  296.7 2.2 copy-start.5
  306.4 3.6 copy-start.6
  314.7 2.2 copy-start.5
  324.4 3.6 copy-start.6
  332.7 2.2 copy-start.5
  342.4 3.6 copy-start.6
  350.7 2.2 copy-start.5
  360.5 3.6 copy-start.6
  378.5 3.6 copy-start.6
  396.5 3.6 copy-start.6
  415.4 228.4 %reduce-scatter.5.cloned.1.call-start = ((), (), s32[]{:S(2)}) async-start(), calls=%async_computation.5 | async-start | bytes 5242880 | tf_op jit(solution)/shard_map/reduce_scatter | solution.py:160
  419.9 5.7 collective-permute-start.15
  (21 other events, 22.3 us)
Sparse Core Ops, SparseCore 0:
  10.4 49.8 all-gather.4
  62.1 41.4 all-gather.2
  415.5 174.7 reduce-scatter.2
  592.8 51.0 reduce-scatter.4
